TPU v7x, 256 devices: a whole 4x4x8 slice. The times are simulated.
256 devices in a mesh: seq: 8 (over y, core), space: 32 (over z, x).
Axes of the slice: x: 4, y: 4, z: 8, core: 2. Of those that a mesh axis runs over, the one named last changes fastest.
Arguments:
- features: bfloat16 [2048, 65536], P(None, ('seq', 'space')), may hold values from -6 to 6
- targets: bfloat16 [2048, 65536], P(None, ('seq', 'space')), may hold values from -6 to 6
- write_keys: bfloat16 [128, 65536], P(None, ('seq', 'space')), may hold values from -0.5 to 0.5
- read_queries: bfloat16 [128, 65536], P(None, ('seq', 'space')), may hold values from -0.0234375 to 0.0234375
- decay_codes: int32 [32, 65536], P('space', 'seq'), may hold values from 0 to 99, as said below
- scan_order: int32 [8192], replicated, may hold values from 0 to 8191, each once
- masked: int32 [49152], P(('seq', 'space')), may hold values from 0 to 65535, as said below
- skip_gain: float32 [32], P('space'), may hold values from 0.5 to 1.5
Outputs:
- mixed: bfloat16 [2048, 65536], P(None, ('seq', 'space'))
- grad_features: bfloat16 [2048, 65536], P(None, ('seq', 'space'))
Inputs may be any that keep to these rules, and one draw needn't show every extreme that they name: `decay_codes`: a token's decay factor for its head is exp(-(0.065536 / 65536) code). `masked`: entries k * 192 to (k + 1) * 192 - 1 are distinct indices among tokens k * 256 to (k + 1) * 256 - 1.
All inputs are finite; a program needn't handle non-finite values.
Results may differ from a plain program's by a relative error of at most 0.0034.
Values may be sent and summed in bfloat16 or wider, within the bound.
No kernel may reach another device: no remote copies, remote signals or barrier semaphores. Data moves between devices by JAX's collectives and lax.ppermute only.
A program may use at most 128 MiB of HBM per device.

v0:
```python
from functools import partial

import jax
import jax.numpy as jnp
from jax import lax
from jax.sharding import PartitionSpec as P

highest = lax.Precision.HIGHEST


def prefix(part, axis, combine, identity, reverse):
    count = lax.axis_size(axis)
    place = lax.axis_index(axis)
    ahead = count - 1 - place if reverse else place
    gathered = jax.tree.map(lambda a: lax.all_gather(a, axis), part)
    state = jax.tree.map(lambda a, e: jnp.zeros_like(a) + jnp.asarray(e, a.dtype), part, identity)

    def one(lap, state):
        source = count - 1 - lap if reverse else lap
        return combine(
            state, jax.tree.map(lambda a: lax.dynamic_index_in_dim(a, source, 0, False), gathered)
        )

    return lax.fori_loop(0, ahead, one, state)


def fading(amount, unit):
    return jnp.exp(-unit * amount.astype(jnp.float32))


def combine(unit, earlier, latter):
    return (earlier[0] + latter[0], earlier[1] * fading(latter[0], unit)[:, None, None] + latter[1])


def block_pass(values, into_state, from_state, running, block_size, unit):
    head_count, head_width, length = values.shape
    state_count = into_state.shape[0]
    block_count = length // block_size
    zero_state = jnp.zeros((head_count, state_count, head_width), jnp.float32)

    def pieces(block_index):
        block_start = block_index * block_size
        value_block = lax.dynamic_slice_in_dim(values, block_start, block_size, 2)
        into_block = lax.dynamic_slice_in_dim(into_state, block_start, block_size, 1)
        from_block = lax.dynamic_slice_in_dim(from_state, block_start, block_size, 1)
        step_block = lax.dynamic_slice_in_dim(running, block_start, block_size, 1)
        earlier = lax.dynamic_slice_in_dim(running, jnp.maximum(block_start - 1, 0), 1, 1)[:, 0]
        earlier = jnp.where(block_index > 0, earlier, jnp.zeros_like(earlier))
        return (value_block, into_block, from_block, step_block, earlier)

    def forward_blocks(state_sum, block_index):
        value_block, into_block, from_block, step_block, earlier = pieces(block_index)
        latest = step_block[:, -1]
        gram_block = jnp.einsum(
            "ns,nt->st", into_block, from_block, preferred_element_type=jnp.float32
        )
        spread = jnp.abs(step_block[:, None, :] - step_block[:, :, None])
        weights = (gram_block[None] * fading(spread, unit)).astype(jnp.bfloat16)
        inside = jnp.einsum(
            "hps,hst->hpt", value_block, weights, preferred_element_type=jnp.float32
        )
        readout = jnp.einsum(
            "hnp,nt->hpt", state_sum, from_block.astype(jnp.float32), precision=highest
        )
        readout = readout * fading(step_block - earlier[:, None], unit)[:, None, :]
        scaled = (
            into_block.astype(jnp.float32)[None]
            * fading(latest[:, None] - step_block, unit)[:, None, :]
        )
        update = jnp.einsum(
            "hns,hps->hnp", scaled, value_block.astype(jnp.float32), precision=highest
        )
        state_sum = state_sum * fading(latest - earlier, unit)[:, None, None] + update
        return (state_sum, inside + readout)

    def reverse_blocks(state_sum, block_index):
        value_block, into_block, from_block, step_block, earlier = pieces(block_index)
        latest = step_block[:, -1]
        readout = jnp.einsum(
            "hnp,nt->hpt", state_sum, from_block.astype(jnp.float32), precision=highest
        )
        readout = readout * fading(latest[:, None] - step_block, unit)[:, None, :]
        scaled = (
            into_block.astype(jnp.float32)[None]
            * fading(step_block - earlier[:, None], unit)[:, None, :]
        )
        update = jnp.einsum(
            "hns,hps->hnp", scaled, value_block.astype(jnp.float32), precision=highest
        )
        state_sum = state_sum * fading(latest - earlier, unit)[:, None, None] + update
        return (state_sum, readout)

    ahead_sum, forward_out = lax.scan(forward_blocks, zero_state, jnp.arange(block_count))
    behind, reverse_out = lax.scan(
        reverse_blocks, zero_state, jnp.arange(block_count), reverse=True
    )
    own_part = jnp.moveaxis(forward_out + reverse_out, 0, 2).reshape(head_count, head_width, length)
    return (own_part, ahead_sum, behind)


def pass_states(totals, ahead_sum, behind, unit):
    joiner = partial(combine, unit)
    identity_pair = (jnp.zeros_like(totals), jnp.zeros_like(ahead_sum))
    from_before = prefix((totals, ahead_sum), "seq", joiner, identity_pair, False)[1]
    from_after = prefix((totals, behind), "seq", joiner, identity_pair, True)[1]
    return (from_before, from_after)


def incoming(from_state, running, totals, from_before, from_after, unit):
    read_wide = from_state.astype(jnp.float32)
    reached = (
        jnp.einsum("hnp,nl->hpl", from_before, read_wide, precision=highest)
        * fading(running, unit)[:, None, :]
    )
    reached = (
        reached
        + jnp.einsum("hnp,nl->hpl", from_after, read_wide, precision=highest)
        * fading(totals[:, None] - running, unit)[:, None, :]
    )
    return reached


def per_device(
    features, targets, write_keys, read_queries, decay_codes, scan_order, masked, skip_gain
):
    space_size = lax.axis_size("space")
    seq_size = lax.axis_size("seq")
    head_count = decay_codes.shape[0]
    tok_dev = features.shape[1]
    unit = 0.065536 / (tok_dev * space_size * seq_size)
    head_width = features.shape[0] // (head_count * space_size)
    first_token = (lax.axis_index("seq") * space_size + lax.axis_index("space")) * tok_dev
    slot_grid = lax.broadcasted_iota(jnp.int32, (masked.shape[0], tok_dev), 1)
    mask_row = jnp.max(
        jnp.where((masked - first_token)[:, None] == slot_grid, 1.0, 0.0), axis=0
    ).astype(jnp.float32)
    head_x = lax.all_to_all(features, "space", split_axis=0, concat_axis=1, tiled=True)
    into_state, from_state = (
        lax.all_gather(write_keys, "space", axis=1, tiled=True),
        lax.all_gather(read_queries, "space", axis=1, tiled=True),
    )
    length = head_x.shape[1]
    block_size = min(512, length)
    reverse_order = (
        jnp.zeros_like(scan_order).at[scan_order].set(jnp.arange(length, dtype=jnp.int32))
    )
    into_state = jnp.take(into_state, scan_order, axis=1)
    from_state = jnp.take(from_state, scan_order, axis=1)
    running = jnp.cumsum(jnp.take(decay_codes, scan_order, axis=1), axis=1)
    totals = running[:, -1].astype(jnp.float32)

    def mixing(values, write_side, read_side):
        own_part, ahead_sum, behind = block_pass(
            values, write_side, read_side, running, block_size, unit
        )
        from_before, from_after = pass_states(totals, ahead_sum, behind, unit)
        reached = incoming(read_side, running, totals, from_before, from_after, unit)
        return own_part + reached + skip_gain[:, None, None] * values.astype(jnp.float32)

    def to_scan(head_rows):
        return jnp.take(head_rows, scan_order, axis=1).reshape(head_count, head_width, length)

    def to_positions(scan_rows):
        return jnp.take(
            scan_rows.reshape(head_count * head_width, length), reverse_order, axis=1
        ).astype(jnp.bfloat16)

    mixed_heads = to_positions(mixing(to_scan(head_x), into_state, from_state))
    mixed = lax.all_to_all(mixed_heads, "space", split_axis=1, concat_axis=0, tiled=True)
    residue = (mask_row[None] * (mixed.astype(jnp.float32) - targets.astype(jnp.float32))).astype(
        jnp.bfloat16
    )
    residue_heads = lax.all_to_all(residue, "space", split_axis=0, concat_axis=1, tiled=True)
    grads_heads = to_positions(mixing(to_scan(residue_heads), from_state, into_state))
    grad_features = lax.all_to_all(grads_heads, "space", split_axis=1, concat_axis=0, tiled=True)
    return (mixed, grad_features)


def solution(mesh):
    return jax.shard_map(
        per_device,
        mesh=mesh,
        in_specs=(
            P(None, ("seq", "space")),
            P(None, ("seq", "space")),
            P(None, ("seq", "space")),
            P(None, ("seq", "space")),
            P("space", "seq"),
            P(),
            P(("seq", "space")),
            P("space"),
        ),
        out_specs=(P(None, ("seq", "space")), P(None, ("seq", "space"))),
        check_vma=False,
    )
```

profile of v0, /device:TPU:2, one launch (start us, length us, event | category | flops | bytes accessed | tf_op | source)
XLA Modules:
  0.0 1129.3 jit_solution(606934662148419698)
XLA Ops:
  10.5 11.6 %all-to-all-start = ((bf16[32,64,256]{2,1,0:T(8,128)(2,1)}), bf16[32,64,256]{2,1,0:T(8,128)(2,1)S(1)}, u32[]{:S(2)}, u32[]{:S(2)}) async-start(bf16[32,64,256]{2,1,0:T(8,128)(2,1)} %bitcast.362), calls=%async_computation | async-start | bytes 2097152 | tf_op jit(solution)/shard_map/all_to_all | solution.py:137
  22.2 45.5 %gather_fusion = s32[8192]{0:T(1024)S(1)} fusion(s32[8192]{0:T(1024)S(1)} %bitcast.351, s32[8192]{0:T(1024)S(1)} %get-tuple-element.1136), kind=kCustom, calls=%fused_computation.6 | custom fusion | bytes 98304 | tf_op jit(solution)/shard_map/jit(_take)/gather | solution.py:149
  71.1 14.9 %all-reduce = f32[8]{0:T(128)S(1)} all-reduce(f32[8]{0:T(128)S(1)} %bitcast_dynamic-update-slice_fusion), channel_id=1, replica_groups=mesh['seq'=8,'space'=32] {'seq'}, use_global_device_ids=true, to_apply=%add | all-reduce | flops 8 | bytes 64
  86.7 30.5 %scatter_custom_fusion = s32[8192]{0:T(1024)S(1)} fusion(s32[8192]{0:T(1024)S(1)} %get-tuple-element.1135, s32[8192]{0:T(1024)S(1)} %iota.21, s32[]{:T(128)} %constant.447.clone.1), kind=kCustom, calls=%fused_computation.177 | custom fusion | bytes 32772 | tf_op jit(solution)/shard_map/scatter | solution.py:145
  118.4 29.2 %gather_fusion.2 = bf16[8192,64]{1,0:T(8,128)(2,1)} fusion(bf16[64,8192]{0,1:T(8,128)(2,1)S(1)} %bitcast.353, s32[8192]{0:T(1024)S(1)} %get-tuple-element.1136), kind=kCustom, calls=%fused_computation.clone | custom fusion | bytes 2129920 | tf_op jit(solution)/shard_map/jit(_take)/gather | solution.py:161
  150.7 29.9 %gather_fusion.3 = bf16[8192,128]{1,0:T(8,128)(2,1)} fusion(bf16[128,8192]{0,1:T(8,128)(2,1)} %all-gather.9.cloned.1.call-done, s32[8192]{0:T(1024)S(1)} %get-tuple-element.1136), kind=kCustom, calls=%fused_computation.4.clone | custom fusion | bytes 4227072 | tf_op jit(solution)/shard_map/jit(_take)/gather | solution.py:148
  180.5 29.9 %gather_fusion.1 = bf16[8192,128]{1,0:T(8,128)(2,1)} fusion(bf16[128,8192]{0,1:T(8,128)(2,1)} %all-gather.7.cloned.1.call-done, s32[8192]{0:T(1024)S(1)} %get-tuple-element.1136), kind=kCustom, calls=%fused_computation.1.clone | custom fusion | bytes 4227072 | tf_op jit(solution)/shard_map/jit(_take)/gather | solution.py:147
  224.9 129.6 %while.114 = (s32[]{:T(128)}, f32[1,128,64]{1,2,0:T(8,128)S(1)}, f32[16,1,64,512]{3,2,1,0:T(8,128)}, s32[16]{0:T(128)S(1)}, s32[1,8192]{1,0:T(1,128)S(1)}, /*ind...) while((s32[]{:T(128)}, f32[1,128,64]{1,2,0:T(8,128)S(1)}, ...), condition=%wide.region_3.6_spmd, body=%wide.region_2.0_spmd.sunk | while | flops 203115536 | bytes 1168741 | solution.py:93
  356.1 106.1 %while.115 = (s32[]{:T(128)}, f32[1,128,64]{1,2,0:T(8,128)S(1)}, f32[16,1,64,512]{3,2,1,0:T(8,128)}, s32[16]{0:T(128)S(1)}, s32[1,8192]{1,0:T(1,128)S(1)}, /*ind...) while((s32[]{:T(128)}, f32[1,128,64]{1,2,0:T(8,128)S(1)}, ...), condition=%wide.region_5.8_spmd, body=%wide.region_4.7_spmd.sunk | while | flops 100846608 | bytes 569209 | solution.py:94
  467.9 13.9 %all-gather = f32[8,128,64]{1,2,0:T(8,128)} all-gather(f32[1,128,64]{1,2,0:T(8,128)S(1)} %get-tuple-element.833), channel_id=2, replica_groups=mesh['seq'=8,'space'=32] {'seq'}, dimensions={0}, use_global_device_ids=true | all-gather | bytes 294912 | tf_op jit(solution)/shard_map/all_gather | solution.py:15
  481.8 26.4 %all-gather.1 = f32[8,128,64]{1,2,0:T(8,128)} all-gather(f32[1,128,64]{1,2,0:T(8,128)S(1)} %get-tuple-element.835), channel_id=3, replica_groups=mesh['seq'=8,'space'=32] {'seq'}, dimensions={0}, use_global_device_ids=true | all-gather | bytes 294912 | tf_op jit(solution)/shard_map/all_gather | solution.py:15
  508.2 19.7 %while.117 = (s32[]{:T(128)}, f32[1,128,64]{2,1,0:T(8,128)S(1)}, s32[]{:T(128)}, f32[8,1]{0,1:T(1,128)}, f32[8,1,128,64]{2,3,0,1:T(8,128)}, /*index=5*/s32[]{:T(128)}, s32[]{:T(128)}, s32[]{:T(128)}, s32[]{:T(128)}) while((s32[]{:T(128)}, f32[1,128,64]{2,1,0:T(8,128)S(1)}, s32[]{:T(128)}, f32[8,1]{0,1:T(1,128)}, ...), condition=%wide.region_9.12_spmd, body=%wide.region_8.11_spmd.sunk | while | flops 16391 | bytes 229551 | solution.py:24
  535.8 29.2 %gather_fusion.4 = bf16[8192,64]{1,0:T(8,128)(2,1)} fusion(bf16[64,8192]{0,1:T(8,128)(2,1)S(1)} %copy.107, s32[8192]{0:T(1024)S(1)} %fusion.107), kind=kCustom, calls=%fused_computation.2.clone | custom fusion | bytes 2129920 | tf_op jit(solution)/shard_map/jit(_take)/gather | solution.py:164
  572.5 9.7 all-to-all-start.1
  582.3 25.6 %all-to-all-done.1 = bf16[64,32,256]{2,0,1:T(8,128)(2,1)S(1)} async-done(((bf16[64,32,256]{2,0,1:T(8,128)(2,1)}), bf16[64,32,256]{2,0,1:T(8,128)(2,1)S(1)}, u32[]{:S(2)}, u32[]{:S(2)}) %all-to-all-start.1) | async-done | bytes 1048608 | tf_op jit(solution)/shard_map/all_to_all | solution.py:169
  614.9 25.4 %all-to-all-done.2 = bf16[32,64,256]{2,1,0:T(8,128)(2,1)S(1)} async-done(((bf16[32,64,256]{2,1,0:T(8,128)(2,1)}), bf16[32,64,256]{2,1,0:T(8,128)(2,1)S(1)}, u32[]{:S(2)}, u32[]{:S(2)}) %all-to-all-start.2) | async-done | bytes 1048608 | tf_op jit(solution)/shard_map/all_to_all | solution.py:173
  641.4 29.2 %gather_fusion.5 = bf16[8192,64]{1,0:T(8,128)(2,1)} fusion(bf16[64,8192]{0,1:T(8,128)(2,1)S(1)} %bitcast.352, s32[8192]{0:T(1024)S(1)} %get-tuple-element.1136), kind=kCustom, calls=%fused_computation.3.clone | custom fusion | bytes 2129920 | tf_op jit(solution)/shard_map/jit(_take)/gather | solution.py:161
  673.9 161.4 %while.118 = (s32[]{:T(128)}, f32[1,128,64]{1,2,0:T(8,128)S(1)}, f32[16,1,64,512]{3,2,1,0:T(8,128)S(1)}, s32[16]{0:T(128)S(1)}, s32[1,8192]{1,0:T(1,128)}, /*ind...) while((s32[]{:T(128)}, f32[1,128,64]{1,2,0:T(8,128)S(1)}, ...), condition=%wide.region_13.17_spmd, body=%wide.region_12.16_spmd.sunk | while | flops 203115536 | bytes 1168741 | solution.py:93
  837.0 144.2 %while.119 = (s32[]{:T(128)}, f32[1,128,64]{1,2,0:T(8,128)S(1)}, f32[16,1,64,512]{3,2,1,0:T(8,128)}, s32[16]{0:T(128)S(1)}, s32[1,8192]{1,0:T(1,128)}, /*index=5...) while((s32[]{:T(128)}, f32[1,128,64]{1,2,0:T(8,128)S(1)}, ...), condition=%wide.region_15.19_spmd, body=%wide.region_14.18_spmd.sunk | while | flops 100846608 | bytes 569209 | solution.py:94
  984.8 13.9 %all-gather.2 = f32[8,128,64]{1,2,0:T(8,128)} all-gather(f32[1,128,64]{1,2,0:T(8,128)S(1)} %get-tuple-element.839), channel_id=4, replica_groups=mesh['seq'=8,'space'=32] {'seq'}, dimensions={0}, use_global_device_ids=true | all-gather | bytes 294912 | tf_op jit(solution)/shard_map/all_gather | solution.py:15
  1002.6 26.4 %all-gather.3 = f32[8,128,64]{1,2,0:T(8,128)} all-gather(f32[1,128,64]{1,2,0:T(8,128)S(1)} %get-tuple-element.841), channel_id=5, replica_groups=mesh['seq'=8,'space'=32] {'seq'}, dimensions={0}, use_global_device_ids=true | all-gather | bytes 294912 | tf_op jit(solution)/shard_map/all_gather | solution.py:15
  1029.0 15.3 %while.121 = (s32[]{:T(128)}, f32[1,128,64]{2,1,0:T(8,128)S(1)}, s32[]{:T(128)}, f32[8,1]{0,1:T(1,128)S(1)}, f32[8,1,128,64]{2,3,0,1:T(8,128)}, /*index=5*/s32[]{:T(128)}, s32[]{:T(128)}, s32[]{:T(128)}, s32[]{:T(128)}) while((s32[]{:T(128)}, f32[1,128,64]{2,1,0:T(8,128)S(1)}, s32[]{:T(128)}, f32[8,1]{0,1:T(1,128)S(1)}, ...), condition=%wide.region_19.23_spmd, body=%wide.region_18.22_spmd.sunk | while | flops 16391 | bytes 229551 | solution.py:24
  1051.9 29.2 %gather_fusion.6 = bf16[8192,64]{1,0:T(8,128)(2,1)} fusion(bf16[64,8192]{0,1:T(8,128)(2,1)S(1)} %copy.120, s32[8192]{0:T(1024)S(1)} %fusion.107), kind=kCustom, calls=%fused_computation.5.clone | custom fusion | bytes 2129920 | tf_op jit(solution)/shard_map/jit(_take)/gather | solution.py:164
  1094.1 26.4 %all-to-all-done.3 = bf16[64,32,256]{2,0,1:T(8,128)(2,1)S(1)} async-done(((bf16[64,32,256]{2,0,1:T(8,128)(2,1)}), bf16[64,32,256]{2,0,1:T(8,128)(2,1)S(1)}, u32[]{:S(2)}, u32[]{:S(2)}) %all-to-all-start.3) | async-done | bytes 1048608 | tf_op jit(solution)/shard_map/all_to_all | solution.py:175
  (543 shorter events, 483.2 us)
Async XLA Ops:
  7.2 15.0 %copy-start = (s32[1,8192]{1,0:T(1,128)S(1)}, s32[1,8192]{1,0:T(1,128)}, u32[]{:S(2)}) copy-start(s32[1,8192]{1,0:T(1,128)} %param.34) | copy-start | bytes 98308
  7.2 14.9 %copy-start.11 = (s32[8192]{0:T(1024)S(1)}, s32[8192]{0:T(1024)}, u32[]{:S(2)}) copy-start(s32[8192]{0:T(1024)} %param.35) | copy-start | bytes 98308
  7.2 143.5 %all-gather.9.cloned.1.call-start = ((), (), s32[]{:S(2)}) async-start(), calls=%async_computation.5 | async-start | bytes 2162688 | tf_op jit(solution)/shard_map/all_gather | solution.py:140
  8.8 171.7 %all-gather.7.cloned.1.call-start = ((), (), s32[]{:S(2)}) async-start(), calls=%async_computation.4 | async-start | bytes 2162688 | tf_op jit(solution)/shard_map/all_gather | solution.py:139
  10.5 106.8 %all-to-all-start = ((bf16[32,64,256]{2,1,0:T(8,128)(2,1)}), bf16[32,64,256]{2,1,0:T(8,128)(2,1)S(1)}, u32[]{:S(2)}, u32[]{:S(2)}) async-start(bf16[32,64,256]{2,1,0:T(8,128)(2,1)} %bitcast.362), calls=%async_computation | async-start | bytes 2097152 | tf_op jit(solution)/shard_map/all_to_all | solution.py:137
  22.2 47.7 %copy-start.13 = (u32[256]{0:T(256)S(1)}, u32[256]{0:T(256)}, u32[]{:S(2)}) copy-start(u32[256]{0:T(256)} %constant.466) | copy-start | bytes 3076
  217.4 3.0 copy-start.2
  462.2 1.4 copy-start.5
  462.2 4.1 copy-start.10
  466.3 61.7 %copy-start.4 = (bf16[128,8192]{0,1:T(8,128)(2,1)S(1)}, bf16[128,8192]{0,1:T(8,128)(2,1)}, u32[]{:S(2)}) copy-start(bf16[128,8192]{0,1:T(8,128)(2,1)} %get-tuple-element.1137) | copy-start | bytes 6291460
  481.8 26.4 %copy-start.14 = (f32[8,1]{0,1:T(1,128)}, f32[8,1]{0,1:T(1,128)S(1)}, u32[]{:S(2)}) copy-start(f32[8,1]{0,1:T(1,128)S(1)} %get-tuple-element.1826) | copy-start | bytes 100
  528.0 2.3 copy-start.8
  570.9 11.3 %copy-start.12 = (s32[192]{0:T(256)S(1)}, s32[192]{0:T(256)}, u32[]{:S(2)}) copy-start(s32[192]{0:T(256)} %param.36) | copy-start | bytes 2308
  570.9 37.1 %copy-start.9 = (bf16[2048,256]{1,0:T(8,128)(2,1)S(1)}, bf16[2048,256]{1,0:T(8,128)(2,1)}, u32[]{:S(2)}) copy-start(bf16[2048,256]{1,0:T(8,128)(2,1)} %param.31) | copy-start | bytes 3145732
  572.5 35.5 %all-to-all-start.1 = ((bf16[64,32,256]{2,0,1:T(8,128)(2,1)}), bf16[64,32,256]{2,0,1:T(8,128)(2,1)S(1)}, u32[]{:S(2)}, u32[]{:S(2)}) async-start(bf16[64,32,256]{2,0,1:T(8,128)(2,1)} %copy.108), calls=%async_computation.1 | async-start | bytes 2097152 | tf_op jit(solution)/shard_map/all_to_all | solution.py:169
  608.0 1.3 copy-start.6
  609.3 31.0 %all-to-all-start.2 = ((bf16[32,64,256]{2,1,0:T(8,128)(2,1)}), bf16[32,64,256]{2,1,0:T(8,128)(2,1)S(1)}, u32[]{:S(2)}, u32[]{:S(2)}) async-start(bf16[32,64,256]{2,1,0:T(8,128)(2,1)} %bitcast.92), calls=%async_computation.2 | async-start | bytes 2097152 | tf_op jit(solution)/shard_map/all_to_all | solution.py:173
  983.3 15.4 %copy-start.15 = (f32[8,1]{0,1:T(1,128)S(1)}, f32[8,1]{0,1:T(1,128)}, u32[]{:S(2)}) copy-start(f32[8,1]{0,1:T(1,128)} %get-tuple-element.1827) | copy-start | bytes 100
  983.3 15.7 %copy-start.3 = (bf16[128,8192]{0,1:T(8,128)(2,1)S(1)}, bf16[128,8192]{0,1:T(8,128)(2,1)}, u32[]{:S(2)}) copy-start(bf16[128,8192]{0,1:T(8,128)(2,1)} %copy-done.2) | copy-start | bytes 6291460
  1086.9 33.6 %copy-start.7 = (bf16[64,32,256]{2,0,1:T(8,128)(2,1)S(1)}, bf16[64,32,256]{2,0,1:T(8,128)(2,1)}, u32[]{:S(2)}) copy-start(bf16[64,32,256]{2,0,1:T(8,128)(2,1)} %copy-done.6) | copy-start | bytes 3145732
  1088.6 32.0 %all-to-all-start.3 = ((bf16[64,32,256]{2,0,1:T(8,128)(2,1)}), bf16[64,32,256]{2,0,1:T(8,128)(2,1)S(1)}, u32[]{:S(2)}, u32[]{:S(2)}) async-start(bf16[64,32,256]{2,0,1:T(8,128)(2,1)} %copy.121), calls=%async_computation.3 | async-start | bytes 2097152 | tf_op jit(solution)/shard_map/all_to_all | solution.py:175
  1120.6 1.9 copy-start.1
Sparse Core Ops, SparseCore 0:
  11.2 80.9 all-gather.8
  94.8 74.9 all-gather.6
where the time goes:
time: 1140 us; the launch traced here: 1130 us
  local copies, waits for them, and re-layouts  403 us (35%)
  matrix products  218 us (19%)
  loops' own time  184 us (16%)
  other arithmetic  104 us (9%)
  blocking collectives  95.4 us (8%)
  waiting for transfers between devices  77.5 us (7%)
  starting transfers between devices  32.5 us (3%)
  between operations  15.9 us (1%)
    another operation x2, loops' own time, block_pass(): lax.scan(reverse_blocks, zero_state, jnp.arange(block_count), reverse=True)  86.8 us
    another operation x2, loops' own time, block_pass(): lax.scan(forward_blocks, zero_state, jnp.arange(block_count))  86.4 us
    all_gather x4, blocking collectives, prefix(): gathered = jax.tree.map(lambda a: lax.all_gather(a, axis), part)  80.6 us
    exp x97, other arithmetic, fading(): return jnp.exp(-unit * amount.astype(jnp.float32))  63.8 us
    gather x4, local copies, waits for them, and re-layouts, to_scan(): jnp.take(head_rows, scan_order, axis=1)  62.3 us
    gather x2, local copies, waits for them, and re-layouts, to_positions(): jnp.take(scan_rows.reshape(head_count * head_width, length), reverse_orde...  58.4 us
    dot_general x32, matrix products, forward_blocks(): jnp.einsum('hps,hst->hpt', value_block, weights, preferred_element_type=j...  51.2 us
    gather x1, local copies, waits for them, and re-layouts, per_device(): running = jnp.cumsum(jnp.take(decay_codes, scan_order, axis=1), axis=1)  45.5 us
  transfers between devices with their start and end apart: 6, of which 3 were waited for; matrix products, arithmetic and copies ran while one was open for 13% of the time, Pallas kernels for 0%

commit v1 on v0

v1 whole, which is shorter than its diff:
```python
from functools import partial

import jax
import jax.numpy as jnp
from jax import lax
from jax.experimental import pallas as pl
from jax.experimental.pallas import tpu as pltpu
from jax.sharding import PartitionSpec as P

BLOCK = 512
ROWS = 16
f32, bf16 = jnp.float32, jnp.bfloat16
vmem = pl.BlockSpec(memory_space=pltpu.VMEM)
smem = pl.BlockSpec(memory_space=pltpu.SMEM)


def call(kernel, outs, ins, scratch, limit, flops, name):
    specs = [smem if s else vmem for _, s in ins]
    args = [a for a, _ in ins]
    moved = sum(a.size * a.dtype.itemsize for a in args)
    moved += sum(o.size * o.dtype.itemsize for o in outs)
    return pl.pallas_call(
        kernel,
        out_shape=outs,
        in_specs=specs,
        out_specs=[vmem] * len(outs),
        scratch_shapes=scratch,
        compiler_params=pltpu.CompilerParams(vmem_limit_bytes=limit << 20),
        cost_estimate=pl.CostEstimate(flops=flops, bytes_accessed=moved, transcendentals=0),
        name=name,
    )(*args)


def struct(shape, dtype):
    return jax.ShapeDtypeStruct(shape, dtype)


def left_half(shape):
    return lax.broadcasted_iota(jnp.int32, shape, 1) < shape[1] // 2


def split(value):
    high = value.astype(bf16)
    return high, (value - high.astype(f32)).astype(bf16)


def gather_rows(order, first, pairs):
    count = pairs[0][1].shape[0] * 8

    def some(j, _):
        for i in range(ROWS):
            row = order[first + j * ROWS + i]
            for src, dst in pairs:
                dst[j * (ROWS // 8) + i // 8, pl.ds(i % 8, 1), :] = src[pl.ds(row, 1), :]
        return 0

    lax.fori_loop(0, count // ROWS, some, 0)


def scatter_rows(order, first, src, dst):
    count = src.shape[0] * 8

    def some(j, _):
        for i in range(ROWS):
            row = order[first + j * ROWS + i]
            dst[pl.ds(row, 1), :] = src[j * (ROWS // 8) + i // 8, pl.ds(i % 8, 1), :]
        return 0

    lax.fori_loop(0, count // ROWS, some, 0)


def sides_kernel(order, gathered, q_out, w_out, qt_out, wt_out, mask_out, q_all, w_all, q_blk, w_blk):
    chunks, blocks = gathered.shape[0], q_out.shape[0]
    tok = (gathered.shape[1] - 16) // 2

    def unpack(c, _):
        base = pl.multiple_of(c * tok, tok)
        w_all[pl.ds(base, tok), :] = gathered[c, 0:tok, :].astype(f32)
        q_all[pl.ds(base, tok), :] = gathered[c, tok : 2 * tok, :].astype(f32)
        mask_out[c] = gathered[c, 2 * tok : 2 * tok + 16, :].astype(f32)[0:8, :]
        return 0

    lax.fori_loop(0, chunks, unpack, 0)

    def block(b, _):
        gather_rows(order, b * BLOCK, [(q_all, q_blk), (w_all, w_blk)])
        q = q_blk[...].reshape(BLOCK, 128)
        w = w_blk[...].reshape(BLOCK, 128)
        q_out[b] = q.astype(bf16)
        w_out[b] = w.astype(bf16)
        qt_out[b] = q.T.astype(bf16)
        wt_out[b] = w.T.astype(bf16)
        return 0

    lax.fori_loop(0, blocks, block, 0)


def states_kernel(unit, residual, order, *refs):
    if residual:
        mixed, targets, mask, codes, into_t, x_out, e_out, p_out, pay_out, x_all, x_blk, tri = refs
    else:
        values, codes, into_t, x_out, e_out, p_out, pay_out, x_all, x_blk, tri = refs
    chunks, width, tok = codes.shape[0], 64, codes.shape[2]
    blocks = x_out.shape[0]

    def load(c, _):
        base = pl.multiple_of(c * tok, tok)
        if residual:
            row = mask[c]
            wide = jnp.concatenate([row[0:1, :], row[1:2, :]], axis=1)
            part = wide * (mixed[c].astype(f32) - targets[c].astype(f32))
            part = part.astype(bf16).astype(f32)
        else:
            part = values[c].astype(f32)
        code = jnp.broadcast_to(codes[c], (width, tok))
        x_all[pl.ds(base, tok), :] = jnp.concatenate([part, code], axis=0).T
        return 0

    lax.fori_loop(0, chunks, load, 0)
    tri[...] = jnp.where(
        lax.broadcasted_iota(jnp.int32, (BLOCK, BLOCK), 0)
        >= lax.broadcasted_iota(jnp.int32, (BLOCK, BLOCK), 1),
        1.0,
        0.0,
    ).astype(bf16)
    total = jnp.sum(codes[...])
    left = left_half((BLOCK, 128))
    rate = jnp.where(left, unit, -unit)

    def block(b, state):
        earlier, summed = state
        gather_rows(order, b * BLOCK, [(x_all, x_blk)])
        x = x_blk[...].reshape(BLOCK, 128)
        reach = jnp.dot(tri[...], x.astype(bf16), preferred_element_type=f32) + earlier
        wide = jnp.where(left, pltpu.roll(reach, 64, 1), reach)
        e = jnp.exp(rate * (wide - 0.5 * total))
        both = jnp.where(left, x, pltpu.roll(x, 64, 1))
        high, low = split(both * e)
        p = jnp.dot(
            into_t[b], jnp.concatenate([high, low], axis=1), preferred_element_type=f32
        )
        p = p[:, :128] + p[:, 128:]
        x_out[b] = both.astype(bf16)
        e_out[b] = e
        p_out[b] = p
        return reach[BLOCK - 1 : BLOCK, :], summed + p

    zero = (jnp.zeros((1, 128), f32), jnp.zeros((128, 128), f32))
    _, summed = lax.fori_loop(0, blocks, block, zero)
    pay_out[0:128, :] = summed
    pay_out[128:136, :] = jnp.full((8, 128), total, f32)


def inside_kernel(from_ref, into_t, x_ref, e_ref, out):
    lower = lax.broadcasted_iota(jnp.int32, (BLOCK, BLOCK), 0) >= lax.broadcasted_iota(
        jnp.int32, (BLOCK, BLOCK), 1
    )

    def block(b, _):
        gram = jnp.dot(from_ref[b], into_t[b], preferred_element_type=f32)
        gram = jnp.where(lower, gram, 0.0).astype(bf16)
        scaled = (x_ref[b].astype(f32) * e_ref[b]).astype(bf16)
        out[b] = jnp.dot(gram, scaled, preferred_element_type=f32)
        return 0

    lax.fori_loop(0, out.shape[0], block, 0)


def finish_kernel(unit, order, where, skip, from_ref, x_ref, e_ref, in_ref, p_ref, others, out, fr, y_blk, y_all):
    blocks, chunks, tok = x_ref.shape[0], out.shape[0], out.shape[2]
    groups = others.shape[0]
    me = where[0]
    gain = skip[0]
    half = left_half((1, 128))
    centers = []
    before = jnp.zeros((1, 128), f32)
    for g in range(groups):
        size = others[g, 128:129, :]
        centers.append(before + 0.5 * size)
        before = before + size
    mine = jnp.zeros((1, 128), f32)
    for g in range(groups):
        mine = mine + jnp.where(me == g, centers[g], 0.0)
    init = jnp.zeros((128, 128), f32)
    for g in range(groups):
        factor = jnp.exp(-unit * jnp.abs(mine - centers[g]))
        ahead = jnp.where(g < me, factor, 0.0)
        behind = jnp.where(g > me, factor, 0.0)
        init = init + others[g, 0:128, :] * jnp.where(half, ahead, behind)
    left = left_half((128, 128))

    def forward(b, run):
        fr[b, :, 0:128] = run
        return run + p_ref[b]

    lax.fori_loop(0, blocks, forward, init)

    def backward(i, run):
        b = blocks - 1 - i
        run = run + p_ref[b]
        high, low = split(jnp.where(left, fr[b, :, 0:128], run))
        fr[b, :, 0:128] = high.astype(f32)
        fr[b, :, 128:256] = low.astype(f32)
        return run

    lax.fori_loop(0, blocks, backward, init)
    wide = left_half((BLOCK, 128))

    def block(b, _):
        read = jnp.dot(from_ref[b], fr[b].astype(bf16), preferred_element_type=f32)
        near = in_ref[b]
        z = read[:, :128] + read[:, 128:] + jnp.where(wide, near, -near)
        z = z * pltpu.roll(e_ref[b], 64, 1)
        y = z + pltpu.roll(z, 64, 1) + gain * x_ref[b].astype(f32)
        y_blk[...] = y.reshape(BLOCK // 8, 8, 128)
        scatter_rows(order, b * BLOCK, y_blk, y_all)
        return 0

    lax.fori_loop(0, blocks, block, 0)

    def store(c, _):
        base = pl.multiple_of(c * tok, tok)
        out[c] = y_all[pl.ds(base, tok), :].T[0:64, :].astype(bf16)
        return 0

    lax.fori_loop(0, chunks, store, 0)


def per_device(
    features, targets, write_keys, read_queries, decay_codes, scan_order, masked, skip_gain
):
    space_size = lax.axis_size("space")
    seq_size = lax.axis_size("seq")
    state = write_keys.shape[0]
    tok = features.shape[1]
    length = tok * space_size
    blocks = length // BLOCK
    unit = 0.065536 / (length * seq_size)
    width = features.shape[0] // space_size
    seq_place = lax.axis_index("seq")
    first_token = (seq_place * space_size + lax.axis_index("space")) * tok

    def swap(a, axis):
        return lax.all_to_all(a, axis, split_axis=0, concat_axis=0, tiled=True)

    head_x = swap(features.reshape(space_size, width, tok), "space")
    slot_grid = lax.broadcasted_iota(jnp.int32, (masked.shape[0], tok), 1)
    mask_row = jnp.max(
        jnp.where((masked - first_token)[:, None] == slot_grid, 1.0, 0.0), axis=0
    ).astype(bf16)
    packet = jnp.concatenate(
        [
            write_keys.T,
            read_queries.T,
            mask_row.reshape(tok // state, state),
            jnp.zeros((16 - tok // state, state), bf16),
        ],
        axis=0,
    )
    gathered = lax.all_gather(packet, "space", axis=0, tiled=False)
    head_targets = swap(targets.reshape(space_size, width, tok), "space")
    codes = decay_codes.astype(f32).reshape(space_size, 1, tok)
    where = seq_place.reshape(1).astype(jnp.int32)

    by_block = struct((blocks, BLOCK, state), bf16)
    by_block_t = struct((blocks, state, BLOCK), bf16)
    wide = struct((blocks, BLOCK, 128), f32)
    small = pltpu.VMEM((BLOCK // 8, 8, 128), f32)
    full = pltpu.VMEM((length, 128), f32)
    q, w, q_t, w_t, mask = call(
        sides_kernel,
        [by_block, by_block, by_block_t, by_block_t, struct((space_size, 8, 128), f32)],
        [(scan_order, True), (gathered, False)],
        [full, full, small, small],
        40,
        10**9,
        "sides",
    )

    def mixing(sources, residual, into_t, from_side):
        x, e, p, pay = call(
            partial(states_kernel, unit, residual),
            [by_block, wide, struct((blocks, state, 128), f32), struct((state + 8, 128), f32)],
            [(scan_order, True), *sources, (codes, False), (into_t, False)],
            [full, small, pltpu.VMEM((BLOCK, BLOCK), bf16)],
            40,
            2 * 10**9,
            "states",
        )
        others = swap(jnp.broadcast_to(pay[None], (seq_size,) + pay.shape), "seq")
        near = call(
            inside_kernel,
            [wide],
            [(from_side, False), (into_t, False), (x, False), (e, False)],
            [],
            40,
            4 * 10**9,
            "inside",
        )[0]
        return call(
            partial(finish_kernel, unit),
            [struct((space_size, width, tok), bf16)],
            [
                (scan_order, True),
                (where, True),
                (skip_gain, True),
                (from_side, False),
                (x, False),
                (e, False),
                (near, False),
                (p, False),
                (others, False),
            ],
            [pltpu.VMEM((blocks, state, 256), f32), small, full],
            40,
            2 * 10**9,
            "finish",
        )[0]

    mixed_heads = mixing([(head_x, False)], False, w_t, q)
    mixed = swap(mixed_heads, "space").reshape(features.shape)
    sources = [(mixed_heads, False), (head_targets, False), (mask, False)]
    grads_heads = mixing(sources, True, q_t, w)
    grad_features = swap(grads_heads, "space").reshape(features.shape)
    return (mixed, grad_features)


def solution(mesh):
    return jax.shard_map(
        per_device,
        mesh=mesh,
        in_specs=(
            P(None, ("seq", "space")),
            P(None, ("seq", "space")),
            P(None, ("seq", "space")),
            P(None, ("seq", "space")),
            P("space", "seq"),
            P(),
            P(("seq", "space")),
            P("space"),
        ),
        out_specs=(P(None, ("seq", "space")), P(None, ("seq", "space"))),
        check_vma=False,
    )
```

time: 1140 us -> 344 us (0.30)
  local copies, waits for them, and re-layouts: 403 us -> 35.4 us
  matrix products: 218 us -> 0 us
  loops' own time: 184 us -> 0 us
  Pallas kernels: 0 us -> 121 us
  other arithmetic: 104 us -> 1.62 us
  blocking collectives: 95.4 us -> 27.9 us
  waiting for transfers between devices: 77.5 us -> 104 us
    gather x9 -> x0, local copies, waits for them, and re-layouts: 226 us -> none  [the longest x4 62.3 us: to_scan(): jnp.take(head_rows, scan_order, axis=1)]
    dot_general x164 -> x0, matrix products: 218 us -> none  [the longest x32 51.2 us: forward_blocks(): jnp.einsum('hps,hst->hpt', value_block, weights, preferred_element_type=j...]
    another operation x8 -> x0, loops' own time: 184 us -> none  [the longest x2 86.8 us: block_pass(): lax.scan(reverse_blocks, zero_state, jnp.arange(block_count), reverse=True)]
    pallas_call x0 -> x7, Pallas kernels: none -> 121 us  [call(): pl.pallas_call(kernel, out_shape=outs, in_specs=specs, out_specs=[vmem] *...]
    all_gather x4 -> x0, blocking collectives: 80.6 us -> none  [prefix(): gathered = jax.tree.map(lambda a: lax.all_gather(a, axis), part)]
    all_gather x2 -> x1, waiting for transfers between devices: 0.01 us -> 75.9 us  [per_device(): gathered = lax.all_gather(packet, 'space', axis=0, tiled=False)]
    exp x97 -> x0, other arithmetic: 63.8 us -> none  [fading(): return jnp.exp(-unit * amount.astype(jnp.float32))]
    slice x66 -> x0, local copies, waits for them, and re-layouts: 63.2 us -> none  [the longest x32 31.7 us: reverse_blocks(): latest = step_block[:, -1]]
  transfers between devices with their start and end apart: 6 -> 5, of which waited for: 3 -> 2; matrix products, arithmetic and copies ran while one was open for 13% -> 0% of each run, Pallas kernels for 0% -> 22%
where the time goes in v1:
time: 344 us; the launch traced here: 343 us
  Pallas kernels  121 us (35%)
  waiting for transfers between devices  104 us (30%)
  starting transfers between devices  38.3 us (11%)
  local copies, waits for them, and re-layouts  35.4 us (10%)
  blocking collectives  27.9 us (8%)
  between operations  14.9 us (4%)
    pallas_call x7, Pallas kernels, call(): pl.pallas_call(kernel, out_shape=outs, in_specs=specs, out_specs=[vmem] *...  121 us
    all_gather x1, waiting for transfers between devices, per_device(): gathered = lax.all_gather(packet, 'space', axis=0, tiled=False)  75.9 us
    all_to_all x4, starting transfers between devices, swap(): return lax.all_to_all(a, axis, split_axis=0, concat_axis=0, tiled=True)  38.3 us
    unnamed x58, local copies, waits for them, and re-layouts  35.3 us
    all_to_all x2, blocking collectives, swap(): return lax.all_to_all(a, axis, split_axis=0, concat_axis=0, tiled=True)  27.9 us
    all_to_all x4, waiting for transfers between devices, swap(): return lax.all_to_all(a, axis, split_axis=0, concat_axis=0, tiled=True)  27.6 us
  transfers between devices with their start and end apart: 5, of which 2 were waited for; matrix products, arithmetic and copies ran while one was open for 0% of the time, Pallas kernels for 22%

profile of v1, /device:TPU:2, one launch (start us, length us, event | category | flops | bytes accessed | tf_op | source)
XLA Modules:
  0.0 342.7 jit_solution(1183106368735403620)
XLA Ops:
  10.9 11.7 %all-to-all-start = ((bf16[32,64,256]{2,1,0:T(8,128)(2,1)}), bf16[32,64,256]{2,1,0:T(8,128)(2,1)}, u32[]{:S(2)}, u32[]{:S(2)}) async-start(bf16[32,64,256]{2,1,0:T(8,128)(2,1)} %bitcast.16), calls=%async_computation | async-start | bytes 2097152 | tf_op jit(solution)/shard_map/all_to_all | solution.py:244
  22.6 75.9 %all-gather.3.cloned.1.call-done = bf16[16896,128]{1,0:T(8,128)(2,1)} async-done(((bf16[528,128]{1,0:T(8,128)(2,1)}), bf16[16896,128]{1,0:T(8,128)(2,1)}) %all-gather.3.cloned.1.call-update) | async-done | bytes 4325392 | tf_op jit(solution)/shard_map/all_gather | solution.py:260
  98.5 2.2 copy-done
  100.7 16.4 %sides.1 = (bf16[16,512,128]{2,1,0:T(8,128)(2,1)S(1)}, bf16[16,512,128]{2,1,0:T(8,128)(2,1)S(1)}, bf16[16,128,512]{2,1,0:T(8,128)(2,1)S(1)}, bf16[16,128,512]{2,1,0:T(8,128)(2,1)S(1)}, f32[32,8,128]{2,1,0:T(8,128)S(1)}) custom-call(s32[8192]{0:T(1024)S(1)} %copy-done.19, bf16[32,528,128]{2,1,0:T(8,128)(2,1)S(1)} %bitcast.12), custom_call_target="tpu_custom_call" | custom-call | flops 1000000000 | bytes 12877824 | tf_op jit(solution)/shard_map/sides/pallas_call | solution.py:22
  121.3 1.6 copy-done.24
  122.9 22.9 %states.2 = (bf16[16,512,128]{2,1,0:T(8,128)(2,1)S(1)}, f32[16,512,128]{2,1,0:T(8,128)S(1)}, f32[16,128,128]{2,1,0:T(8,128)S(1)}, f32[136,128]{1,0:T(8,128)S(1)}) custom-call(s32[8192]{0:T(1024)S(1)} %copy-done.19, bf16[32,64,256]{2,1,0:T(8,128)(2,1)} %all-to-all-done.refs_0_, f32[32,1,256]{2,1,0:T(1,128)S(1)} %bitcast.13, bf16[16,128,512]{2,1,0:T(8,128)(2,1)S(1)} %copy-done.24), custom_call_target="tpu_custom_call" | custom-call | flops 2000000000 | bytes 10620928 | tf_op jit(solution)/shard_map/states/pallas_call | solution.py:22
  145.8 2.0 copy-done.3
  150.1 14.8 %all_to_all.30.others = f32[8,136,128]{2,1,0:T(8,128)S(1)} all-to-all(f32[8,136,128]{2,1,0:T(8,128)S(1)} %broadcast_in_dim.27), channel_id=1, replica_groups=mesh['seq'=8,'space'=32] {'seq'}, dimensions={0} | all-to-all | bytes 1114112 | tf_op jit(solution)/shard_map/all_to_all | solution.py:244
  164.9 7.0 %all-to-all-start.3 = ((bf16[32,64,256]{2,1,0:T(8,128)(2,1)}), bf16[32,64,256]{2,1,0:T(8,128)(2,1)}, u32[]{:S(2)}, u32[]{:S(2)}) async-start(bf16[32,64,256]{2,1,0:T(8,128)(2,1)} %bitcast.17), calls=%async_computation.3 | async-start | bytes 2097152 | tf_op jit(solution)/shard_map/all_to_all | solution.py:244
  174.2 1.6 copy-done.14
  177.4 9.1 %inside.2.in_ref = f32[16,512,128]{2,1,0:T(8,128)S(1)} custom-call(bf16[16,512,128]{2,1,0:T(8,128)(2,1)S(1)} %copy-done.8, bf16[16,128,512]{2,1,0:T(8,128)(2,1)S(1)} %copy-done.25, bf16[16,512,128]{2,1,0:T(8,128)(2,1)S(1)} %copy-done.14, f32[16,512,128]{2,1,0:T(8,128)} %copy-done.3), custom_call_target="tpu_custom_call" | custom-call | flops 4000000000 | bytes 14680064 | tf_op jit(solution)/shard_map/inside/pallas_call | solution.py:22
  186.5 2.0 copy-done.6
  188.5 20.1 %finish.2.refs_0_ = bf16[32,64,256]{2,1,0:T(8,128)(2,1)} custom-call(s32[8192]{0:T(1024)S(1)} %copy-done.19, s32[1]{0:T(128)} %bitcast.where, f32[1]{0:T(128)S(6)} %copy.19.skip, bf16[16,512,128]{2,1,0:T(8,128)(2,1)S(1)} %copy-done.9, bf16[16,512,128]{2,1,0:T(8,128)(2,1)S(1)} %copy-done.14, f32[16,512,128]{2,1,0:T(8,128)S(1)} %copy-done.4, ...), custom_call_target="tpu_custom_call" | custom-call | flops 2000000000 | bytes 15269896 | tf_op jit(solution)/shard_map/finish/pallas_call | solution.py:22
  208.6 1.6 copy-done.21
  210.2 23.4 %states.3 = (bf16[16,512,128]{2,1,0:T(8,128)(2,1)S(1)}, f32[16,512,128]{2,1,0:T(8,128)S(1)}, f32[16,128,128]{2,1,0:T(8,128)S(1)}, f32[136,128]{1,0:T(8,128)S(1)}) custom-call(s32[8192]{0:T(1024)S(1)} %copy-done.19, bf16[32,64,256]{2,1,0:T(8,128)(2,1)} %finish.2.refs_0_, bf16[32,64,256]{2,1,0:T(8,128)(2,1)} %all-to-all-done.3.refs_1_, ...), custom_call_target="tpu_custom_call" | custom-call | flops 2000000000 | bytes 11800576 | tf_op jit(solution)/shard_map/states/pallas_call | solution.py:22
  233.6 2.0 copy-done.1
  237.9 13.1 %all_to_all.31.others = f32[8,136,128]{2,1,0:T(8,128)S(1)} all-to-all(f32[8,136,128]{2,1,0:T(8,128)S(1)} %broadcast_in_dim.28), channel_id=1, replica_groups=mesh['seq'=8,'space'=32] {'seq'}, dimensions={0} | all-to-all | bytes 1114112 | tf_op jit(solution)/shard_map/all_to_all | solution.py:244
  251.0 9.8 %all-to-all-start.2 = ((bf16[32,64,256]{2,1,0:T(8,128)(2,1)}), bf16[32,64,256]{2,1,0:T(8,128)(2,1)}, u32[]{:S(2)}, u32[]{:S(2)}) async-start(bf16[32,64,256]{2,1,0:T(8,128)(2,1)} %finish.2.refs_0_), calls=%async_computation.2 | async-start | bytes 2097152 | tf_op jit(solution)/shard_map/all_to_all | solution.py:244
  264.0 9.1 %inside.3.in_ref = f32[16,512,128]{2,1,0:T(8,128)S(1)} custom-call(bf16[16,512,128]{2,1,0:T(8,128)(2,1)S(1)} %get-tuple-element.21.from_ref, bf16[16,128,512]{2,1,0:T(8,128)(2,1)S(1)} %copy-done.22, bf16[16,512,128]{2,1,0:T(8,128)(2,1)S(1)} %copy-done.11, f32[16,512,128]{2,1,0:T(8,128)} %copy-done.1), custom_call_target="tpu_custom_call" | custom-call | flops 4000000000 | bytes 14680064 | tf_op jit(solution)/shard_map/inside/pallas_call | solution.py:22
  273.2 2.0 copy-done.5
  275.2 20.1 %finish.3 = bf16[32,64,256]{2,1,0:T(8,128)(2,1)} custom-call(s32[8192]{0:T(1024)S(1)} %copy-done.19, s32[1]{0:T(128)} %bitcast.where, f32[1]{0:T(128)S(6)} %copy.19.skip, bf16[16,512,128]{2,1,0:T(8,128)(2,1)S(1)} %get-tuple-element.21.from_ref, bf16[16,512,128]{2,1,0:T(8,128)(2,1)S(1)} %copy-done.12, f32[16,512,128]{2,1,0:T(8,128)S(1)} %copy-done.2, ...), custom_call_target="tpu_custom_call" | custom-call | flops 2000000000 | bytes 15269896 | tf_op jit(solution)/shard_map/finish/pallas_call | solution.py:22
  295.3 9.8 %all-to-all-start.5 = ((bf16[32,64,256]{2,1,0:T(8,128)(2,1)}), bf16[32,64,256]{2,1,0:T(8,128)(2,1)S(1)}, u32[]{:S(2)}, u32[]{:S(2)}) async-start(bf16[32,64,256]{2,1,0:T(8,128)(2,1)} %finish.3), calls=%async_computation.5 | async-start | bytes 2097152 | tf_op jit(solution)/shard_map/all_to_all | solution.py:244
  305.1 27.6 %all-to-all-done.5 = bf16[32,64,256]{2,1,0:T(8,128)(2,1)S(1)} async-done(((bf16[32,64,256]{2,1,0:T(8,128)(2,1)}), bf16[32,64,256]{2,1,0:T(8,128)(2,1)S(1)}, u32[]{:S(2)}, u32[]{:S(2)}) %all-to-all-start.5) | async-done | bytes 1048608 | tf_op jit(solution)/shard_map/all_to_all | solution.py:244
  332.7 2.3 copy.20
  (62 shorter events, 19.9 us)
Async XLA Ops:
  7.2 15.4 %copy-start.26 = (s32[1,8192]{1,0:T(1,128)S(1)}, s32[1,8192]{1,0:T(1,128)}, u32[]{:S(2)}) copy-start(s32[1,8192]{1,0:T(1,128)} %param.12) | copy-start | bytes 98308
  7.2 91.3 %copy-start.19 = (s32[8192]{0:T(1024)S(1)}, s32[8192]{0:T(1024)}, u32[]{:S(2)}) copy-start(s32[8192]{0:T(1024)} %order.9) | copy-start | bytes 98308
  7.2 91.3 %all-gather.3.cloned.1.call-start = ((), (), s32[]{:S(2)}) async-start(), calls=%async_computation.6 | async-start | bytes 4460544 | tf_op jit(solution)/shard_map/all_gather | solution.py:260
  10.9 110.4 %all-to-all-start = ((bf16[32,64,256]{2,1,0:T(8,128)(2,1)}), bf16[32,64,256]{2,1,0:T(8,128)(2,1)}, u32[]{:S(2)}, u32[]{:S(2)}) async-start(bf16[32,64,256]{2,1,0:T(8,128)(2,1)} %bitcast.16), calls=%async_computation | async-start | bytes 2097152 | tf_op jit(solution)/shard_map/all_to_all | solution.py:244
  98.5 2.2 copy-start
  121.3 1.6 copy-start.24
  145.8 2.0 copy-start.3
  164.9 43.7 %all-to-all-start.3 = ((bf16[32,64,256]{2,1,0:T(8,128)(2,1)}), bf16[32,64,256]{2,1,0:T(8,128)(2,1)}, u32[]{:S(2)}, u32[]{:S(2)}) async-start(bf16[32,64,256]{2,1,0:T(8,128)(2,1)} %bitcast.17), calls=%async_computation.3 | async-start | bytes 2097152 | tf_op jit(solution)/shard_map/all_to_all | solution.py:244
  172.6 1.6 copy-start.8
  174.2 1.6 copy-start.14
  175.8 1.6 copy-start.25
  177.4 11.2 %copy-start.4 = (f32[16,512,128]{2,1,0:T(8,128)S(1)}, f32[16,512,128]{2,1,0:T(8,128)}, u32[]{:S(2)}) copy-start(f32[16,512,128]{2,1,0:T(8,128)} %copy-done.3) | copy-start | bytes 12582916
  177.4 11.2 %copy-start.9 = (bf16[16,512,128]{2,1,0:T(8,128)(2,1)S(1)}, bf16[16,512,128]{2,1,0:T(8,128)(2,1)}, u32[]{:S(2)}) copy-start(bf16[16,512,128]{2,1,0:T(8,128)(2,1)} %copy-done.7) | copy-start | bytes 6291460
  177.4 11.2 %copy-start.18 = (f32[16,128,128]{2,1,0:T(8,128)S(1)}, f32[16,128,128]{2,1,0:T(8,128)}, u32[]{:S(2)}) copy-start(f32[16,128,128]{2,1,0:T(8,128)} %copy-done.17) | copy-start | bytes 3145732
  186.5 2.0 copy-start.6
  208.6 1.6 copy-start.21
  233.6 2.0 copy-start.1
  251.0 44.3 %all-to-all-start.2 = ((bf16[32,64,256]{2,1,0:T(8,128)(2,1)}), bf16[32,64,256]{2,1,0:T(8,128)(2,1)}, u32[]{:S(2)}, u32[]{:S(2)}) async-start(bf16[32,64,256]{2,1,0:T(8,128)(2,1)} %finish.2.refs_0_), calls=%async_computation.2 | async-start | bytes 2097152 | tf_op jit(solution)/shard_map/all_to_all | solution.py:244
  260.8 1.6 copy-start.11
  264.0 11.2 %copy-start.2 = (f32[16,512,128]{2,1,0:T(8,128)S(1)}, f32[16,512,128]{2,1,0:T(8,128)}, u32[]{:S(2)}) copy-start(f32[16,512,128]{2,1,0:T(8,128)} %copy-done.1) | copy-start | bytes 12582916
  264.0 11.2 %copy-start.12 = (bf16[16,512,128]{2,1,0:T(8,128)(2,1)S(1)}, bf16[16,512,128]{2,1,0:T(8,128)(2,1)}, u32[]{:S(2)}) copy-start(bf16[16,512,128]{2,1,0:T(8,128)(2,1)} %copy-done.10) | copy-start | bytes 6291460
  264.0 11.2 %copy-start.16 = (f32[16,128,128]{2,1,0:T(8,128)S(1)}, f32[16,128,128]{2,1,0:T(8,128)}, u32[]{:S(2)}) copy-start(f32[16,128,128]{2,1,0:T(8,128)} %copy-done.15) | copy-start | bytes 3145732
  273.2 2.0 copy-start.5
  295.3 37.4 %all-to-all-start.5 = ((bf16[32,64,256]{2,1,0:T(8,128)(2,1)}), bf16[32,64,256]{2,1,0:T(8,128)(2,1)S(1)}, u32[]{:S(2)}, u32[]{:S(2)}) async-start(bf16[32,64,256]{2,1,0:T(8,128)(2,1)} %finish.3), calls=%async_computation.5 | async-start | bytes 2097152 | tf_op jit(solution)/shard_map/all_to_all | solution.py:244
  (8 other events, 10.4 us)
Sparse Core Ops, SparseCore 0:
  11.2 87.2 all-gather.2
